TPU v7x, 768 devices: a whole 4x8x12 slice. The times are simulated.
768 devices in a mesh: energy: 96 (over x, z, core), atom: 8 (over y).
Axes of the slice: x: 4, y: 8, z: 12, core: 2. Of those that a mesh axis runs over, the one named last changes fastest.
Arguments:
- green_blocks: bfloat16 [192, 16, 2, 256, 256], P('energy', 'atom'), may hold values from -6 to 6
- coupling: bfloat16 [16, 256, 256], P('atom'), may hold values from -0.375 to 0.375
- up_partner: int32 [192], P('energy'), may hold values from -1 to 191, as said below
- down_partner: int32 [192], P('energy'), may hold values from -1 to 189, as said below
- up_weight: float32 [192], P('energy'), may hold values from 0.3 to 1.2
- down_weight: float32 [192], P('energy'), may hold values from 0.3 to 1.2
- neighbours: int32 [16, 5], replicated, may hold values from -1 to 15, as said below
- strength: float32 [16, 5], replicated, may hold values from 0.3 to 1
Outputs:
- updated: bfloat16 [192, 16, 2, 256, 256], P('energy', 'atom')
Inputs may be any that keep to these rules, and one draw needn't show every extreme that they name: up_partner[e] = e + k with 2 <= k <= 4, or -1 only where such an e + k would pass the last energy point; k = 4 for some e. down_partner[e] = e - k with 2 <= k <= 4, or -1 only where such an e - k would fall below 0; k = 4 for some e. neighbours[a, j] is a + j - 2 or -1; it is -1 where a + j - 2 lies outside the clusters, and for j = 1, 2, 3 it is -1 nowhere else.
All inputs are finite; a program needn't handle non-finite values.
Results may differ from a plain program's by a relative error of at most 0.023.
Values may be sent and summed in bfloat16 or wider, within the bound.
A program may use at most 32 MiB of HBM per device.

v0:
```python
import jax
import jax.numpy as jnp
from jax import lax
from jax.sharding import PartitionSpec as P


def from_behind(value, axis, by):
    count = lax.axis_size(axis)
    pairs = [(i, i + by) for i in range(count) if 0 <= i + by < count]
    return lax.ppermute(value, axis, pairs)


def complex_product(left, right):

    def single(first, second):
        return jnp.einsum("ecij,ecjk->ecik", first, second, preferred_element_type=jnp.float32)

    real_part = single(left[:, :, 0], right[:, :, 0]) - single(left[:, :, 1], right[:, :, 1])
    imag_part = single(left[:, :, 0], right[:, :, 1]) + single(left[:, :, 1], right[:, :, 0])
    return jnp.stack([real_part, imag_part], axis=2)


def partner_rows(partner, weight, near_block, far_block, near_first, far_first, energy_count):
    near_count = near_block.shape[0]
    present = partner >= 0
    near_mask = (partner >= near_first) & (partner < near_first + near_count)
    near_rows = jnp.take(near_block, jnp.clip(partner - near_first, 0, near_count - 1), axis=0)
    far_rows = jnp.take(far_block, jnp.clip(partner - far_first, 0, energy_count - 1), axis=0)
    factor = jnp.where(present, weight, jnp.float32(0.0))
    chosen = jnp.where(near_mask[:, None, None, None, None], near_rows, far_rows)
    return factor[:, None, None, None, None] * chosen.astype(jnp.float32)


def weighted(weights, sources):
    summed = None
    for column in range(sources.shape[1]):
        piece = weights[:, column][None, :, None, None, None] * sources[
            :, column : column + 1
        ].astype(jnp.float32)
        summed = piece if summed is None else summed + piece
    return summed


def on_device(
    green_blocks, coupling, up_partner, down_partner, up_weight, down_weight, neighbours, strength
):
    energy_count = green_blocks.shape[0]
    cluster_count = green_blocks.shape[1]
    orbitals = green_blocks.shape[-1]
    clusters_all = neighbours.shape[0]
    first_energy = lax.axis_index("energy") * energy_count
    above_blocks = []
    below_blocks = []
    for stride in (1, 2):
        above_blocks.append(from_behind(green_blocks, "energy", -stride))
        below_blocks.append(from_behind(green_blocks, "energy", stride))
    upper_term = partner_rows(
        up_partner,
        up_weight,
        above_blocks[0],
        above_blocks[1],
        first_energy + energy_count,
        first_energy + 2 * energy_count,
        energy_count,
    )
    lower_term = partner_rows(
        down_partner,
        down_weight,
        below_blocks[0],
        below_blocks[1],
        first_energy - energy_count,
        first_energy - 2 * energy_count,
        energy_count,
    )
    hidden = (upper_term + lower_term).astype(jnp.bfloat16)
    columns = jnp.arange(clusters_all, dtype=jnp.int32)
    coupling_table = jnp.sum(
        strength[:, :, None]
        * (neighbours[:, :, None] == columns[None, None, :]).astype(jnp.float32),
        axis=1,
    )
    padded = jnp.pad(coupling_table, cluster_count)
    atom_index = lax.axis_index("atom")

    def table_block(row_device, column_device, width):
        return lax.dynamic_slice(
            padded,
            ((row_device + 1) * cluster_count, (column_device + 1) * cluster_count),
            (cluster_count, width * cluster_count),
        )

    own_term = weighted(table_block(atom_index, atom_index, 1), hidden)
    lower_part = weighted(table_block(atom_index - 1, atom_index, 1), hidden)
    upper_part = weighted(table_block(atom_index + 1, atom_index, 1), hidden)
    from_above = from_behind(lower_part.astype(jnp.bfloat16), "atom", -1).astype(lower_part.dtype)
    from_below = from_behind(upper_part.astype(jnp.bfloat16), "atom", 1).astype(upper_part.dtype)
    reader_total = own_term + from_above + from_below
    reader_sum = reader_total.astype(jnp.bfloat16)
    prefactor = 1.0 / (2.0 * orbitals)
    half_product = jnp.einsum(
        "aij,eacjk->eacik", coupling, reader_sum, preferred_element_type=jnp.float32
    ).astype(jnp.bfloat16)
    self_energy = (
        jnp.einsum("eacij,akj->eacik", half_product, coupling, preferred_element_type=jnp.float32)
        * prefactor
    ).astype(jnp.bfloat16)
    first_term = complex_product(self_energy, green_blocks).astype(jnp.bfloat16)
    second_term = complex_product(green_blocks, first_term)
    second_rounded = second_term.astype(jnp.bfloat16)
    third_term = complex_product(second_rounded, first_term)
    return (green_blocks.astype(jnp.float32) + second_term + third_term).astype(jnp.bfloat16)


def solution(mesh):
    in_specs = (
        P("energy", "atom", None, None, None),
        P("atom", None, None),
        P("energy"),
        P("energy"),
        P("energy"),
        P("energy"),
        P(),
        P(),
    )
    out_specs = P("energy", "atom", None, None, None)
    return jax.shard_map(
        on_device, mesh=mesh, in_specs=in_specs, out_specs=out_specs, check_vma=False
    )
```

profile of v0, /device:TPU:63, one launch (start us, length us, event | category | flops | bytes accessed | tf_op | source)
XLA Modules:
  0.0 106.7 jit_solution(10651598056988066077)
XLA Ops:
  0.0 4.7 %collective-permute-start.2 = (bf16[2,2,2,256,256]{4,3,2,1,0:T(8,128)(2,1)}, bf16[2,2,2,256,256]{4,3,2,1,0:T(8,128)(2,1)S(1)}, u32[]{:S(2)}, u32[]{:S(2)}) collective-permute-start(bf16[2,2,2,256,256]{4,3,2,1,0:T(8,128)(2,1)} %param.10), channel_id=1, source_target_pairs={{0,8},{8,16},{16,24},{24,32},{32,40},{40,48},{48,56},{56,64},{64,7... | collective-permute-start | bytes 3145736 | tf_op jit(solution)/shard_map/ppermute | solution.py:10
  4.7 4.0 %collective-permute-start.3 = (bf16[2,2,2,256,256]{4,3,2,1,0:T(8,128)(2,1)}, bf16[2,2,2,256,256]{4,3,2,1,0:T(8,128)(2,1)S(1)}, u32[]{:S(2)}, u32[]{:S(2)}) collective-permute-start(bf16[2,2,2,256,256]{4,3,2,1,0:T(8,128)(2,1)} %param.10), channel_id=1, source_target_pairs={{0,16},{8,24},{16,32},{24,40},{32,48},{40,56},{48,64},{56,72},{64,... | collective-permute-start | bytes 3145736 | tf_op jit(solution)/shard_map/ppermute | solution.py:10
  8.7 1.9 %collective-permute-start = (bf16[2,2,2,256,256]{4,3,2,1,0:T(8,128)(2,1)}, bf16[2,2,2,256,256]{4,3,2,1,0:T(8,128)(2,1)S(1)}, u32[]{:S(2)}, u32[]{:S(2)}) collective-permute-start(bf16[2,2,2,256,256]{4,3,2,1,0:T(8,128)(2,1)} %param.10), channel_id=1, source_target_pairs={{8,0},{16,8},{24,16},{32,24},{40,32},{48,40},{56,48},{64,56},{72,6... | collective-permute-start | bytes 3145736 | tf_op jit(solution)/shard_map/ppermute | solution.py:10
  10.6 10.5 %collective-permute-start.1 = (bf16[2,2,2,256,256]{4,3,2,1,0:T(8,128)(2,1)}, bf16[2,2,2,256,256]{4,3,2,1,0:T(8,128)(2,1)}, u32[]{:S(2)}, u32[]{:S(2)}) collective-permute-start(bf16[2,2,2,256,256]{4,3,2,1,0:T(8,128)(2,1)} %param.10), channel_id=1, source_target_pairs={{16,0},{24,8},{32,16},{40,24},{48,32},{56,40},{64,48},{72,56},{80,... | collective-permute-start | bytes 3145736 | tf_op jit(solution)/shard_map/ppermute | solution.py:10
  21.2 0.8 select_reduce_fusion
  22.1 0.7 compare_and_fusion.1
  22.7 0.7 compare_and_fusion.3
  23.6 0.7 compare_select_fusion.4
  24.4 1.1 %collective-permute-done.2 = bf16[2,2,2,256,256]{4,3,2,1,0:T(8,128)(2,1)S(1)} collective-permute-done((bf16[2,2,2,256,256]{4,3,2,1,0:T(8,128)(2,1)}, bf16[2,2,2,256,256]{4,3,2,1,0:T(8,128)(2,1)S(1)}, u32[]{:S(2)}, u32[]{:S(2)}) %collective-permute-start.2) | collective-permute-done | bytes 1048608 | tf_op jit(solution)/shard_map/ppermute | solution.py:10
  25.5 1.0 copy-done.4
  26.4 1.8 %gather_fusion.2 = bf16[2,2,2,256,256]{4,3,2,1,0:T(8,128)(2,1)S(1)} fusion(bf16[2,2,2,256,256]{4,3,2,1,0:T(8,128)(2,1)} %copy-done.4, s32[1024]{0:T(1024)S(1)} %get-tuple-element.40), kind=kCustom, calls=%fused_computation.2.clone | custom fusion | bytes 2097160 | tf_op jit(solution)/shard_map/jit(_take)/gather | solution.py:27
  28.3 21.3 %collective-permute-done.3 = bf16[2,2,2,256,256]{4,3,2,1,0:T(8,128)(2,1)S(1)} collective-permute-done((bf16[2,2,2,256,256]{4,3,2,1,0:T(8,128)(2,1)}, bf16[2,2,2,256,256]{4,3,2,1,0:T(8,128)(2,1)S(1)}, u32[]{:S(2)}, u32[]{:S(2)}) %collective-permute-start.3) | collective-permute-done | bytes 1048608 | tf_op jit(solution)/shard_map/ppermute | solution.py:10
  49.6 1.0 copy-done.3
  50.5 1.8 %gather_fusion.3 = bf16[2,2,2,256,256]{4,3,2,1,0:T(8,128)(2,1)S(1)} fusion(bf16[2,2,2,256,256]{4,3,2,1,0:T(8,128)(2,1)} %copy-done.3, s32[1024]{0:T(1024)S(1)} %get-tuple-element.39), kind=kCustom, calls=%fused_computation.3.clone | custom fusion | bytes 2097160 | tf_op jit(solution)/shard_map/jit(_take)/gather | solution.py:28
  52.4 1.0 copy-done.2
  53.4 1.8 %gather_fusion = bf16[2,2,2,256,256]{4,3,2,1,0:T(8,128)(2,1)S(1)} fusion(bf16[2,2,2,256,256]{4,3,2,1,0:T(8,128)(2,1)} %copy-done.2, s32[1024]{0:T(1024)S(1)} %get-tuple-element.42), kind=kCustom, calls=%fused_computation.clone | custom fusion | bytes 2097160 | tf_op jit(solution)/shard_map/jit(_take)/gather | solution.py:27
  55.2 2.8 %gather_fusion.1 = bf16[2,2,2,256,256]{4,3,2,1,0:T(8,128)(2,1)} fusion(bf16[2,2,2,256,256]{4,3,2,1,0:T(8,128)(2,1)} %collective-permute-done.1, s32[1024]{0:T(1024)S(1)} %get-tuple-element.41), kind=kCustom, calls=%fused_computation.1.clone | custom fusion | bytes 2097160 | tf_op jit(solution)/shard_map/jit(_take)/gather | solution.py:28
  58.0 1.9 %add_convert_fusion.3 = bf16[2,2,2,256,256]{4,3,2,1,0:T(8,128)(2,1)S(1)} fusion(bf16[2,2,2,256,256]{4,3,2,1,0:T(8,128)(2,1)S(1)} %gather_fusion.3, bf16[2,2,2,256,256]{4,3,2,1,0:T(8,128)(2,1)S(1)} %gather_fusion.2, bf16[2,2,2,256,256]{4,3,2,1,0:T(8,128)(2,1)} %gather_fusion.1, bf16[2,2,2,256,256]{4,3,2,1,0:T(8,128)(2,1)S(1)} %gather_fusion, ...), kind=kLoop, calls=%fused_computation.11 | loop fusion | flops 6291456 | bytes 5242908 | tf_op jit(solution)/shard_map/convert_element_type | solution.py:75
  60.4 1.3 %copy.53 = f32[2,2,256,256]{2,3,1,0:T(8,128)} copy(f32[2,2,256,256]{3,2,1,0:T(8,128)S(1)} %get-tuple-element.25) | data formatting | bytes 2097152 | tf_op jit(solution)/shard_map/mul | solution.py:37
  61.7 3.2 %add_convert_fusion.2 = (bf16[2,2,2,256,256]{3,4,2,0,1:T(8,128)(2,1)}, bf16[2,2,2,256,256]{3,4,2,0,1:T(8,128)(2,1)}) fusion(f32[2]{0:T(128)S(1)} %get-tuple-element.37, f32[2]{0:T(128)S(1)} %get-tuple-element.38, f32[2,2,256,256]{2,3,1,0:T(8,128)} %copy.53, f32[2,2,256,256]{2,3,1,0:T(8,128)S(1)} %copy.52, f32[2]{0:T(128)S(1)} %get-tuple-element.11, ...), kind=kLoop, calls=%fused_computation.10 | loop fusion | flops 4194304 | bytes 4194336 | tf_op jit(solution)/shard_map/convert_element_type | solution.py:95
  65.0 4.0 %collective-permute-start.4 = (bf16[2,2,2,256,256]{3,4,2,0,1:T(8,128)(2,1)}, bf16[2,2,2,256,256]{3,4,2,0,1:T(8,128)(2,1)}, u32[]{:S(2)}, u32[]{:S(2)}) collective-permute-start(bf16[2,2,2,256,256]{3,4,2,0,1:T(8,128)(2,1)} %get-tuple-element.20), channel_id=1, source_target_pairs={{1,0},{2,1},{3,2},{4,3},{5,4},{6,5},{7,6},{9,8},{10,9},{11,10},{12... | collective-permute-start | bytes 3145736 | tf_op jit(solution)/shard_map/ppermute | solution.py:10
  69.0 1.3 %collective-permute-start.5 = (bf16[2,2,2,256,256]{3,4,2,0,1:T(8,128)(2,1)}, bf16[2,2,2,256,256]{3,4,2,0,1:T(8,128)(2,1)}, u32[]{:S(2)}, u32[]{:S(2)}) collective-permute-start(bf16[2,2,2,256,256]{3,4,2,0,1:T(8,128)(2,1)} %get-tuple-element.21), channel_id=1, source_target_pairs={{0,1},{1,2},{2,3},{3,4},{4,5},{5,6},{6,7},{8,9},{9,10},{10,11},{11... | collective-permute-start | bytes 3145736 | tf_op jit(solution)/shard_map/ppermute | solution.py:10
  70.3 0.5 copy.51
  71.0 19.5 %collective-permute-done.4 = bf16[2,2,2,256,256]{3,4,2,0,1:T(8,128)(2,1)} collective-permute-done((bf16[2,2,2,256,256]{3,4,2,0,1:T(8,128)(2,1)}, bf16[2,2,2,256,256]{3,4,2,0,1:T(8,128)(2,1)}, u32[]{:S(2)}, u32[]{:S(2)}) %collective-permute-start.4) | collective-permute-done | bytes 1048608 | tf_op jit(solution)/shard_map/ppermute | solution.py:10
  90.5 5.1 %collective-permute-done.5 = bf16[2,2,2,256,256]{3,4,2,0,1:T(8,128)(2,1)} collective-permute-done((bf16[2,2,2,256,256]{3,4,2,0,1:T(8,128)(2,1)}, bf16[2,2,2,256,256]{3,4,2,0,1:T(8,128)(2,1)}, u32[]{:S(2)}, u32[]{:S(2)}) %collective-permute-start.5) | collective-permute-done | bytes 1048608 | tf_op jit(solution)/shard_map/ppermute | solution.py:10
  95.6 3.9 %fusion.7 = bf16[2,2,2,256,256]{4,3,2,0,1:T(8,128)(2,1)} fusion(bf16[2,2,2,256,256]{3,4,2,0,1:T(8,128)(2,1)} %collective-permute-done.5, bf16[2,2,2,256,256]{3,4,2,0,1:T(8,128)(2,1)} %collective-permute-done.4, f32[2,2,256,256]{2,3,1,0:T(8,128)} %copy.53, f32[2]{0:T(128)S(1)} %get-tuple-element.7, f32[2,2,256,256]{2,3,1,0:T(8,128)S(1)} %copy.52, ...), kind=kOutput, calls=%fused_computation.25 | convolution fusion | flops 542638080 | bytes 5505040 | tf_op jit(solution)/shard_map/eacij,akj->eacik/dot_general | solution.py:104
  99.5 1.3 %slice_bitcast_fusion.2 = (bf16[2,2,256,256]{3,2,0,1:T(8,128)(2,1)S(1)}, bf16[2,2,256,256]{3,2,0,1:T(8,128)(2,1)S(1)}) fusion(bf16[2,2,2,256,256]{4,3,2,0,1:T(8,128)(2,1)} %fusion.7), kind=kLoop, calls=%fused_computation.36 | loop fusion | bytes 2097152 | tf_op jit(solution)/shard_map/squeeze | solution.py:18
  103.0 0.3 fusion.5
  103.9 0.3 fusion.32
  104.2 0.3 fusion.4
  104.9 0.5 fusion
  105.4 1.3 %copy.73 = bf16[2,2,2,256,256]{4,3,2,1,0:T(8,128)(2,1)} copy(bf16[2,2,2,256,256]{3,4,1,0,2:T(8,128)(2,1)S(1)} %fusion) | data formatting | bytes 2097152 | tf_op jit(solution)/shard_map/convert_element_type | solution.py:111
  (26 shorter events, 4.1 us)
Async XLA Ops:
  0.0 95.6 %copy-start = (bf16[2,256,256]{2,1,0:T(8,128)(2,1)S(1)}, bf16[2,256,256]{2,1,0:T(8,128)(2,1)}, u32[]{:S(2)}) copy-start(bf16[2,256,256]{2,1,0:T(8,128)(2,1)} %param.11) | copy-start | bytes 786436
  0.0 25.5 %collective-permute-start.2 = (bf16[2,2,2,256,256]{4,3,2,1,0:T(8,128)(2,1)}, bf16[2,2,2,256,256]{4,3,2,1,0:T(8,128)(2,1)S(1)}, u32[]{:S(2)}, u32[]{:S(2)}) collective-permute-start(bf16[2,2,2,256,256]{4,3,2,1,0:T(8,128)(2,1)} %param.10), channel_id=1, source_target_pairs={{0,8},{8,16},{16,24},{24,32},{32,40},{40,48},{48,56},{56,64},{64,7... | collective-permute-start | bytes 3145736 | tf_op jit(solution)/shard_map/ppermute | solution.py:10
  4.7 44.9 %collective-permute-start.3 = (bf16[2,2,2,256,256]{4,3,2,1,0:T(8,128)(2,1)}, bf16[2,2,2,256,256]{4,3,2,1,0:T(8,128)(2,1)S(1)}, u32[]{:S(2)}, u32[]{:S(2)}) collective-permute-start(bf16[2,2,2,256,256]{4,3,2,1,0:T(8,128)(2,1)} %param.10), channel_id=1, source_target_pairs={{0,16},{8,24},{16,32},{24,40},{32,48},{40,56},{48,64},{56,72},{64,... | collective-permute-start | bytes 3145736 | tf_op jit(solution)/shard_map/ppermute | solution.py:10
  8.7 43.7 %collective-permute-start = (bf16[2,2,2,256,256]{4,3,2,1,0:T(8,128)(2,1)}, bf16[2,2,2,256,256]{4,3,2,1,0:T(8,128)(2,1)S(1)}, u32[]{:S(2)}, u32[]{:S(2)}) collective-permute-start(bf16[2,2,2,256,256]{4,3,2,1,0:T(8,128)(2,1)} %param.10), channel_id=1, source_target_pairs={{8,0},{16,8},{24,16},{32,24},{40,32},{48,40},{56,48},{64,56},{72,6... | collective-permute-start | bytes 3145736 | tf_op jit(solution)/shard_map/ppermute | solution.py:10
  10.6 44.6 %collective-permute-start.1 = (bf16[2,2,2,256,256]{4,3,2,1,0:T(8,128)(2,1)}, bf16[2,2,2,256,256]{4,3,2,1,0:T(8,128)(2,1)}, u32[]{:S(2)}, u32[]{:S(2)}) collective-permute-start(bf16[2,2,2,256,256]{4,3,2,1,0:T(8,128)(2,1)} %param.10), channel_id=1, source_target_pairs={{16,0},{24,8},{32,16},{40,24},{48,32},{56,40},{64,48},{72,56},{80,... | collective-permute-start | bytes 3145736 | tf_op jit(solution)/shard_map/ppermute | solution.py:10
  25.5 1.0 copy-start.4
  49.6 1.0 copy-start.3
  52.4 1.0 copy-start.2
  61.7 8.5 %copy-start.1 = (bf16[2,2,2,256,256]{4,3,2,1,0:T(8,128)(2,1)S(1)}, bf16[2,2,2,256,256]{4,3,2,1,0:T(8,128)(2,1)}, u32[]{:S(2)}) copy-start(bf16[2,2,2,256,256]{4,3,2,1,0:T(8,128)(2,1)} %param.10) | copy-start | bytes 3145732
  65.0 25.5 %collective-permute-start.4 = (bf16[2,2,2,256,256]{3,4,2,0,1:T(8,128)(2,1)}, bf16[2,2,2,256,256]{3,4,2,0,1:T(8,128)(2,1)}, u32[]{:S(2)}, u32[]{:S(2)}) collective-permute-start(bf16[2,2,2,256,256]{3,4,2,0,1:T(8,128)(2,1)} %get-tuple-element.20), channel_id=1, source_target_pairs={{1,0},{2,1},{3,2},{4,3},{5,4},{6,5},{7,6},{9,8},{10,9},{11,10},{12... | collective-permute-start | bytes 3145736 | tf_op jit(solution)/shard_map/ppermute | solution.py:10
  69.0 26.7 %collective-permute-start.5 = (bf16[2,2,2,256,256]{3,4,2,0,1:T(8,128)(2,1)}, bf16[2,2,2,256,256]{3,4,2,0,1:T(8,128)(2,1)}, u32[]{:S(2)}, u32[]{:S(2)}) collective-permute-start(bf16[2,2,2,256,256]{3,4,2,0,1:T(8,128)(2,1)} %get-tuple-element.21), channel_id=1, source_target_pairs={{0,1},{1,2},{2,3},{3,4},{4,5},{5,6},{6,7},{8,9},{9,10},{10,11},{11... | collective-permute-start | bytes 3145736 | tf_op jit(solution)/shard_map/ppermute | solution.py:10
where the time goes:
time: 107 us
  waiting for transfers between devices  47 us (44%)
  starting transfers between devices  26.4 us (25%)
  local copies, waits for them, and re-layouts  16.5 us (15%)
  other arithmetic  8.76 us (8%)
  matrix products  7.81 us (7%)
    ppermute x6, waiting for transfers between devices, from_behind(): return lax.ppermute(value, axis, pairs)  47 us
    ppermute x6, starting transfers between devices, from_behind(): return lax.ppermute(value, axis, pairs)  26.4 us
    gather x2, local copies, waits for them, and re-layouts, partner_rows(): jnp.take(far_block, jnp.clip(partner - far_first, 0, energy_count - 1), a...  4.64 us
    dot_general x12, matrix products, single(): jnp.einsum('ecij,ecjk->ecik', first, second, preferred_element_type=jnp.f...  3.96 us
    dot_general x1, matrix products, on_device(): jnp.einsum('eacij,akj->eacik', half_product, coupling, preferred_element_...  3.86 us
    gather x2, local copies, waits for them, and re-layouts, partner_rows(): jnp.take(near_block, jnp.clip(partner - near_first, 0, near_count - 1), a...  3.67 us
    unnamed x11, local copies, waits for them, and re-layouts  3.44 us
    convert_element_type x1, other arithmetic, on_device(): lower_part.astype(jnp.bfloat16)  3.22 us
  transfers between devices with their start and end apart: 6, of which 4 were waited for; matrix products, arithmetic and copies ran while one was open for 9% of the time, Pallas kernels for 0%

commit v1 on v0

v1 whole, which is shorter than its diff:
```python
import functools

import jax
import jax.numpy as jnp
from jax import lax
from jax.experimental import pallas as pl
from jax.experimental.pallas import tpu as pltpu
from jax.sharding import PartitionSpec as P

MESH = pl.DeviceIdType.MESH
CHUNKS = 4
F32 = jnp.float32
BF16 = jnp.bfloat16

TO_LOW, TO_HIGH, OWN, PASSED, TO_UNDER, TO_OVER = range(6)


def kernel(
    energy_devices,
    atom_devices,
    green_hbm,
    coupling_hbm,
    up_hbm,
    down_hbm,
    up_weight_hbm,
    down_weight_hbm,
    neighbours_hbm,
    strength_hbm,
    out_hbm,
    *scratch,
):
    chunks = CHUNKS
    orbitals = green_hbm.shape[-1]
    rows = orbitals // chunks
    names = iter(scratch)

    def take(count):
        return [next(names) for _ in range(count)]

    raw_z = take(chunks)
    raw_y = take(chunks)
    summed_z = [take(chunks) for _ in range(2)]
    summed_y = [take(chunks) for _ in range(2)]
    own_sum = [take(chunks) for _ in range(2)]
    hidden = take(chunks)
    sent_y = [take(chunks) for _ in range(2)]
    (
        green,
        coupling,
        up,
        down,
        up_weight,
        down_weight,
        neighbours,
        strength,
        reader,
        x_big,
        gc,
        y_big,
        f_big,
        second_cat,
        result,
        raw_send,
        raw_recv,
        sum_send,
        sum_recv,
        local_sem,
        out_sem,
    ) = names

    d = lax.axis_index("energy")
    y = lax.axis_index("atom")
    core = lax.rem(d, 2)
    low = lax.rem(d + energy_devices - 2, energy_devices)
    high = lax.rem(d + 2, energy_devices)
    partner = d + 1 - 2 * core
    under = lax.rem(y + atom_devices - 1, atom_devices)
    over = lax.rem(y + 1, atom_devices)
    targets = {
        TO_LOW: (low, y),
        TO_HIGH: (high, y),
        OWN: (partner, y),
        PASSED: (partner, y),
        TO_UNDER: (d, under),
        TO_OVER: (d, over),
    }
    slot_of = {TO_LOW: 6, TO_HIGH: 0, OWN: 2 + 2 * core, PASSED: 4 - 2 * core}
    passed_from = 6 - 6 * core

    def remote(source, target, send, recv, kind):
        return pltpu.make_async_remote_copy(
            src_ref=source,
            dst_ref=target,
            send_sem=send,
            recv_sem=recv,
            device_id=targets[kind],
            device_id_type=MESH,
        )

    def raw_copy(kind, r):
        send, recv = raw_send.at[kind, r], raw_recv.at[kind, r]
        if kind in (TO_UNDER, TO_OVER):
            source = green_hbm.at[:, :, 1, pl.ds(r * rows, rows), :]
            side = 1 if kind == TO_UNDER else 0
            return remote(source, raw_y[r].at[side], send, recv, kind)
        target = raw_z[r].at[pl.ds(slot_of[kind], 2)]
        if kind == PASSED:
            source = raw_z[r].at[pl.ds(passed_from, 2)]
        else:
            source = green_hbm.at[:, :, 0, pl.ds(r * rows, rows), :]
        return remote(source, target, send, recv, kind)

    def sum_copy(kind, a, r):
        index = a * chunks + r
        send, recv = sum_send.at[kind, index], sum_recv.at[kind, index]
        if kind in (TO_UNDER, TO_OVER):
            side = 1 if kind == TO_UNDER else 0
            return remote(
                sent_y[a][r].at[1 - side], summed_y[a][r].at[side], send, recv, kind
            )
        target = summed_z[a][r].at[pl.ds(slot_of[kind], 2)]
        if kind == PASSED:
            source = summed_z[a][r].at[pl.ds(passed_from, 2)]
        else:
            source = own_sum[a][r]
        return remote(source, target, send, recv, kind)

    locals_ = [
        pltpu.make_async_copy(source, target, local_sem.at[i])
        for i, (source, target) in enumerate(
            (
                (coupling_hbm, coupling),
                (green_hbm, green),
                (up_hbm, up),
                (down_hbm, down),
                (up_weight_hbm, up_weight),
                (down_weight_hbm, down_weight),
                (neighbours_hbm, neighbours),
                (strength_hbm, strength),
            )
        )
    ]
    for copy in locals_:
        copy.start()

    barrier = pltpu.get_barrier_semaphore()
    for kind in (TO_LOW, TO_HIGH, OWN, TO_UNDER, TO_OVER):
        pl.semaphore_signal(barrier, inc=1, device_id=targets[kind], device_id_type=MESH)
    pl.semaphore_wait(barrier, 5)

    for r in range(chunks):
        for kind in (TO_LOW, TO_HIGH, TO_UNDER, TO_OVER, OWN):
            raw_copy(kind, r).start()

    for copy in locals_:
        copy.wait()

    clusters = 2 * atom_devices
    first_energy = 2 * d
    first_cluster = 2 * y

    def table(a, b):
        row = lax.rem(a + clusters, clusters)
        inside = (a >= 0) & (a < clusters) & (b >= 0) & (b < clusters)
        total = jnp.float32(0.0)
        for j in range(neighbours.shape[0]):
            total = total + jnp.where(neighbours[j, row] == b, strength[j, row], jnp.float32(0.0))
        return jnp.where(inside, total, jnp.float32(0.0))

    def entry(a, b):
        return table(first_cluster + a, first_cluster + b)

    reach = {
        (a, b): entry(a, b) for a in range(-2, 4) for b in range(-2, 4)
        if abs(a - b) <= 2 and (0 <= a < 2 or 0 <= b < 2)
    }

    up_slot, down_slot, up_factor, down_factor = [], [], [], []
    for e in range(2):
        u, l = up[e], down[e]
        up_slot.append(jnp.minimum(jnp.maximum(u - first_energy + 2, 4), 7))
        down_slot.append(jnp.minimum(jnp.maximum(l - first_energy + 4, 0), 3))
        up_factor.append(jnp.where(u >= 0, up_weight[e], jnp.float32(0.0)))
        down_factor.append(jnp.where(l >= 0, down_weight[e], jnp.float32(0.0)))

    def dot(left, right):
        return jnp.dot(left, right, preferred_element_type=F32)

    scale = 1.0 / (2.0 * orbitals)
    for a in range(2):
        turned = coupling[a].T
        for e in range(2):
            for part in range(2):
                x = dot(turned, green[e, a, part]) * scale
                x_big[a, e, 0:orbitals, part * orbitals : (part + 1) * orbitals] = x.astype(BF16)
                other = -x if part == 1 else x
                x_big[a, e, orbitals:, (1 - part) * orbitals : (2 - part) * orbitals] = other.astype(BF16)
                gc[a, e, :, part * orbitals : (part + 1) * orbitals] = dot(
                    green[e, a, part], coupling[a]
                ).astype(BF16)

    def wide(value):
        return value.astype(F32)

    def cluster_sums(r):
        span = pl.ds(r * rows, rows)
        for e in range(2):
            terms = {
                -2: wide(raw_y[r][0, e, 0]),
                -1: wide(raw_y[r][0, e, 1]),
                0: wide(green[e, 0, 1, span, :]),
                1: wide(green[e, 1, 1, span, :]),
                2: wide(raw_y[r][1, e, 0]),
                3: wide(raw_y[r][1, e, 1]),
            }
            for a in range(2):
                total = None
                for b in range(a - 2, a + 3):
                    piece = reach[a, b] * terms[b]
                    total = piece if total is None else total + piece
                own_sum[a][r][e] = total.astype(BF16)

    def energy_sums(r):
        for e in range(2):
            values = []
            for c in range(2):
                value = (
                    up_factor[e] * wide(raw_z[r][up_slot[e], c])
                    + down_factor[e] * wide(raw_z[r][down_slot[e], c])
                ).astype(BF16)
                hidden[r][e, c] = value
                values.append(wide(value))
            sent_y[0][r][0, e] = (reach[-2, 0] * values[0]).astype(BF16)
            sent_y[1][r][0, e] = (reach[-1, 0] * values[0] + reach[-1, 1] * values[1]).astype(BF16)
            sent_y[0][r][1, e] = (reach[2, 0] * values[0] + reach[2, 1] * values[1]).astype(BF16)
            sent_y[1][r][1, e] = (reach[3, 1] * values[1]).astype(BF16)

    def energy_sum_send(a, r):
        for kind in (TO_UNDER, TO_OVER):
            sum_copy(kind, a, r).start()

    def cluster_sum_send(a, r):
        for kind in (TO_LOW, TO_HIGH, OWN):
            sum_copy(kind, a, r).start()

    def raw_second(r):
        raw_copy(OWN, r).wait_recv()
        raw_copy(PASSED, r).wait_recv()
        energy_sums(r)
        energy_sum_send(0, r)

    for r in range(chunks):
        raw_copy(TO_LOW, r).wait_recv()
        raw_copy(TO_HIGH, r).wait_recv()
        raw_copy(PASSED, r).start()
        if r:
            raw_second(r - 1)
        raw_copy(TO_UNDER, r).wait_recv()
        raw_copy(TO_OVER, r).wait_recv()
        cluster_sums(r)
        cluster_sum_send(0, r)
    for r in range(chunks):
        cluster_sum_send(1, r)
    raw_second(chunks - 1)
    for r in range(chunks):
        energy_sum_send(1, r)

    def read(a, r):
        span = pl.ds(r * rows, rows)
        for kind in (TO_UNDER, TO_OVER):
            sum_copy(kind, a, r).wait_recv()
        for e in range(2):
            total = wide(summed_y[a][r][0, e]) + wide(summed_y[a][r][1, e])
            for c in range(2):
                total = total + reach[a, c] * wide(hidden[r][e, c])
            reader[a, e, :, 0:orbitals] = total.astype(BF16)
        for kind in (OWN, PASSED):
            sum_copy(kind, a, r).wait_recv()
        for e in range(2):
            total = up_factor[e] * wide(summed_z[a][r][up_slot[e]]) + down_factor[e] * wide(
                summed_z[a][r][down_slot[e]]
            )
            reader[a, e, :, orbitals:] = total.astype(BF16)
        for e in range(2):
            value = dot(reader[a, e], x_big[a, e])
            real, imag = value[:, :orbitals].astype(BF16), value[:, orbitals:].astype(BF16)
            after = pl.ds(orbitals + r * rows, rows)
            y_big[a, e, span, 0:orbitals] = real
            y_big[a, e, span, orbitals:] = imag
            y_big[a, e, after, 0:orbitals] = -imag
            y_big[a, e, after, orbitals:] = real

    def finish(a):
        for e in range(2):
            first = dot(coupling[a], y_big[a, e, 0:orbitals])
            real, imag = first[:, :orbitals].astype(BF16), first[:, orbitals:].astype(BF16)
            f_big[e, 0:orbitals, 0:orbitals] = real
            f_big[e, 0:orbitals, orbitals:] = imag
            f_big[e, orbitals:, 0:orbitals] = -imag
            f_big[e, orbitals:, orbitals:] = real
        for e in range(2):
            second_cat[e] = dot(gc[a, e], y_big[a, e])
        for e in range(2):
            third = dot(second_cat[e].astype(BF16), f_big[e])
            for part in range(2):
                side = slice(part * orbitals, (part + 1) * orbitals)
                result[a, e, part] = (
                    wide(green[e, a, part]) + second_cat[e, :, side] + third[:, side]
                ).astype(BF16)
        for e in range(2):
            out_copy(a, e).start()

    def out_copy(a, e):
        return pltpu.make_async_copy(result.at[a, e], out_hbm.at[e, a], out_sem.at[a, e])

    steps = [(a, r) for a in range(2) for r in range(chunks)]
    for at, (a, r) in enumerate(steps):
        sum_copy(TO_LOW, a, r).wait_recv()
        sum_copy(TO_HIGH, a, r).wait_recv()
        sum_copy(PASSED, a, r).start()
        if at:
            read(*steps[at - 1])
            if steps[at - 1][1] == chunks - 1:
                finish(steps[at - 1][0])
    read(*steps[-1])
    finish(1)

    for r in range(chunks):
        for kind in range(6):
            raw_copy(kind, r).wait_send()
            for a in range(2):
                sum_copy(kind, a, r).wait_send()
    for a in range(2):
        for e in range(2):
            out_copy(a, e).wait()


def solution(mesh):
    energy_devices, atom_devices = mesh.shape["energy"], mesh.shape["atom"]

    def on_device(
        green_blocks, coupling, up_partner, down_partner, up_weight, down_weight, neighbours, strength
    ):
        orbitals = green_blocks.shape[-1]
        rows = orbitals // CHUNKS
        slots = neighbours.shape[1]
        clusters = neighbours.shape[0]

        def vmem(*shape, dtype=BF16):
            return pltpu.VMEM(shape, dtype)

        many = range(CHUNKS)
        scratch = (
            [vmem(8, 2, rows, orbitals) for _ in many]
            + [vmem(2, 2, 2, rows, orbitals) for _ in many]
            + [vmem(8, rows, orbitals) for _ in range(2 * CHUNKS)]
            + [vmem(2, 2, rows, orbitals) for _ in range(2 * CHUNKS)]
            + [vmem(2, rows, orbitals) for _ in range(2 * CHUNKS)]
            + [vmem(2, 2, rows, orbitals) for _ in many]
            + [vmem(2, 2, rows, orbitals) for _ in range(2 * CHUNKS)]
            + [
                vmem(2, 2, 2, orbitals, orbitals),
                vmem(2, orbitals, orbitals),
                pltpu.SMEM((2,), jnp.int32),
                pltpu.SMEM((2,), jnp.int32),
                pltpu.SMEM((2,), F32),
                pltpu.SMEM((2,), F32),
                pltpu.SMEM((slots, clusters), jnp.int32),
                pltpu.SMEM((slots, clusters), F32),
                vmem(2, 2, rows, 2 * orbitals),
                vmem(2, 2, 2 * orbitals, 2 * orbitals),
                vmem(2, 2, orbitals, 2 * orbitals),
                vmem(2, 2, 2 * orbitals, 2 * orbitals),
                vmem(2, 2 * orbitals, 2 * orbitals),
                vmem(2, orbitals, 2 * orbitals, dtype=F32),
                vmem(2, 2, 2, orbitals, orbitals),
                pltpu.SemaphoreType.DMA((6, CHUNKS)),
                pltpu.SemaphoreType.DMA((6, CHUNKS)),
                pltpu.SemaphoreType.DMA((6, 2 * CHUNKS)),
                pltpu.SemaphoreType.DMA((6, 2 * CHUNKS)),
                pltpu.SemaphoreType.DMA((8,)),
                pltpu.SemaphoreType.DMA((2, 2)),
            ]
        )
        return pl.pallas_call(
            functools.partial(kernel, energy_devices, atom_devices),
            out_shape=jax.ShapeDtypeStruct(green_blocks.shape, green_blocks.dtype),
            in_specs=[pl.BlockSpec(memory_space=pl.ANY)] * 8,
            out_specs=pl.BlockSpec(memory_space=pl.ANY),
            scratch_shapes=scratch,
            compiler_params=pltpu.CompilerParams(
                collective_id=0, has_side_effects=True, vmem_limit_bytes=60 * 1024 * 1024
            ),
            name="update",
        )(
            green_blocks,
            coupling,
            up_partner,
            down_partner,
            up_weight,
            down_weight,
            neighbours.T,
            strength.T,
        )

    in_specs = (
        P("energy", "atom", None, None, None),
        P("atom", None, None),
        P("energy"),
        P("energy"),
        P("energy"),
        P("energy"),
        P(),
        P(),
    )
    out_specs = P("energy", "atom", None, None, None)
    return jax.shard_map(
        on_device, mesh=mesh, in_specs=in_specs, out_specs=out_specs, check_vma=False
    )
```

time: 107 us -> 50.1 us (0.47)
  the two profiles are of different devices: /device:TPU:63 before, /device:TPU:1 now
where the time goes in v1:
time: 50.1 us; the launch traced here: 50 us
  Pallas kernels  47.7 us (95%)
  local copies, waits for them, and re-layouts  2.26 us (5%)
    pallas_call x1, Pallas kernels, on_device(): pl.pallas_call(functools.partial(kernel, energy_devices, atom_devices), o...  47.7 us
    unnamed x1, local copies, waits for them, and re-layouts  2.26 us

profile of v1, /device:TPU:1, one launch (start us, length us, event | category | flops | bytes accessed | tf_op | source)
XLA Modules:
  0.0 50.0 jit_solution(5723702660024838370)
XLA Ops:
  0.0 47.7 %update.1 = bf16[2,2,2,256,256]{4,3,2,1,0:T(8,128)(2,1)} custom-call(bf16[2,2,2,256,256]{4,3,2,1,0:T(8,128)(2,1)} %green_hbm.1, bf16[2,256,256]{2,1,0:T(8,128)(2,1)} %coupling_hbm.1, s32[2]{0:T(128)} %up_hbm.1, s32[2]{0:T(128)} %down_hbm.1, f32[2]{0:T(128)} %up_weight_hbm.1, f32[2]{0:T(128)} %down_weight_hbm.1, s32[5,16]{1,0:T(8,128)} %bitcast.2, ...), custom_call_target="tpu_custom_call" | custom-call | tf_op jit(solution)/shard_map/update/pallas_call | solution.py:385
  47.7 2.3 %copy.10 = bf16[2,2,2,256,256]{4,3,2,1,0:T(8,128)(2,1)} copy(bf16[2,2,2,256,256]{4,3,2,1,0:T(8,128)(2,1)} %update.1) | data formatting | bytes 2097152

commit v2 on v1

--- a/solution.py
+++ b/solution.py
@@ -9,10 +9,14 @@
 
 MESH = pl.DeviceIdType.MESH
 CHUNKS = 4
+ROW = 24
 F32 = jnp.float32
 BF16 = jnp.bfloat16
 
 TO_LOW, TO_HIGH, OWN, PASSED, TO_UNDER, TO_OVER = range(6)
+OVER_Z = (TO_LOW, TO_HIGH, OWN)
+OVER_Y = (TO_UNDER, TO_OVER)
+scope = jax.named_scope
 
 
 def kernel(
@@ -26,7 +30,7 @@
     down_weight_hbm,
     neighbours_hbm,
     strength_hbm,
-    out_hbm,
+    out_ref,
     *scratch,
 ):
     chunks = CHUNKS
@@ -59,33 +63,71 @@
         y_big,
         f_big,
         second_cat,
-        result,
         raw_send,
         raw_recv,
         sum_send,
         sum_recv,
         local_sem,
-        out_sem,
+        ready,
     ) = names
 
     d = lax.axis_index("energy")
     y = lax.axis_index("atom")
     core = lax.rem(d, 2)
-    low = lax.rem(d + energy_devices - 2, energy_devices)
-    high = lax.rem(d + 2, energy_devices)
+    has_low, has_high = d >= 2, d < energy_devices - 2
+    has_under, has_over = y >= 1, y < atom_devices - 1
+    exists = {
+        TO_LOW: has_low,
+        TO_HIGH: has_high,
+        OWN: d >= 0,
+        TO_UNDER: has_under,
+        TO_OVER: has_over,
+    }
     partner = d + 1 - 2 * core
-    under = lax.rem(y + atom_devices - 1, atom_devices)
-    over = lax.rem(y + 1, atom_devices)
     targets = {
-        TO_LOW: (low, y),
-        TO_HIGH: (high, y),
+        TO_LOW: (d - 2, y),
+        TO_HIGH: (d + 2, y),
         OWN: (partner, y),
         PASSED: (partner, y),
-        TO_UNDER: (d, under),
-        TO_OVER: (d, over),
+        TO_UNDER: (d, y - 1),
+        TO_OVER: (d, y + 1),
     }
+    place = lax.rem(d, ROW)
+    never = d < 0
+    first = (d == 0) & (y == 0)
+    leads = {
+        TO_LOW: never,
+        TO_HIGH: first | (place >= ROW - 2),
+        OWN: first,
+        TO_UNDER: never,
+        TO_OVER: first,
+    }
+    late = {
+        TO_LOW: ((d == 2) & (y == 0)) | ((place < 2) & (d >= ROW)),
+        TO_HIGH: never,
+        OWN: (d == 1) & (y == 0),
+        TO_UNDER: (d == 0) & (y == 1),
+        TO_OVER: never,
+    }
+    meets_z = late[TO_LOW] | late[OWN]
+    slow_high = (place >= ROW - 2) & has_high
+    late_z = meets_z | slow_high
+    early_core = jnp.where(slow_high, 1, 0)
+    late_y = late[TO_UNDER]
+    pass_out = jnp.where(core == 0, d < energy_devices - 2, d >= 2)
+    pass_in = jnp.where(core == 0, d >= 2, d < energy_devices - 2)
     slot_of = {TO_LOW: 6, TO_HIGH: 0, OWN: 2 + 2 * core, PASSED: 4 - 2 * core}
     passed_from = 6 - 6 * core
+    kept_from = 6 * core
+
+    barrier = pltpu.get_barrier_semaphore()
+    count = jnp.int32(0)
+    for kind in (TO_LOW, TO_HIGH, OWN, TO_UNDER, TO_OVER):
+        count = count + jnp.where(exists[kind], 1, 0) - jnp.where(late[kind], 1, 0)
+
+        @pl.when(exists[kind] & jnp.logical_not(leads[kind]))
+        def _(kind=kind):
+            pl.semaphore_signal(barrier, inc=1, device_id=targets[kind], device_id_type=MESH)
 
     def remote(source, target, send, recv, kind):
         return pltpu.make_async_remote_copy(
@@ -100,14 +142,14 @@
     def raw_copy(kind, r):
         send, recv = raw_send.at[kind, r], raw_recv.at[kind, r]
         if kind in (TO_UNDER, TO_OVER):
-            source = green_hbm.at[:, :, 1, pl.ds(r * rows, rows), :]
+            source = green.at[:, :, 1, pl.ds(r * rows, rows), :]
             side = 1 if kind == TO_UNDER else 0
             return remote(source, raw_y[r].at[side], send, recv, kind)
         target = raw_z[r].at[pl.ds(slot_of[kind], 2)]
         if kind == PASSED:
             source = raw_z[r].at[pl.ds(passed_from, 2)]
         else:
-            source = green_hbm.at[:, :, 0, pl.ds(r * rows, rows), :]
+            source = green.at[:, :, 0, pl.ds(r * rows, rows), :]
         return remote(source, target, send, recv, kind)
 
     def sum_copy(kind, a, r):
@@ -125,12 +167,20 @@
             source = own_sum[a][r]
         return remote(source, target, send, recv, kind)
 
+    def raw_arrival(r, start, which):
+        place = raw_z[r].at[pl.ds(start, 2)]
+        return remote(place, place, raw_send.at[which, r], raw_recv.at[which, r], OWN)
+
+    def sum_arrival(a, r, start, which):
+        place, index = summed_z[a][r].at[pl.ds(start, 2)], a * chunks + r
+        return remote(place, place, sum_send.at[which, index], sum_recv.at[which, index], OWN)
+
     locals_ = [
         pltpu.make_async_copy(source, target, local_sem.at[i])
         for i, (source, target) in enumerate(
             (
+                (green_hbm, green),
                 (coupling_hbm, coupling),
-                (green_hbm, green),
                 (up_hbm, up),
                 (down_hbm, down),
                 (up_weight_hbm, up_weight),
@@ -143,17 +193,39 @@
     for copy in locals_:
         copy.start()
 
-    barrier = pltpu.get_barrier_semaphore()
-    for kind in (TO_LOW, TO_HIGH, OWN, TO_UNDER, TO_OVER):
-        pl.semaphore_signal(barrier, inc=1, device_id=targets[kind], device_id_type=MESH)
-    pl.semaphore_wait(barrier, 5)
-
-    for r in range(chunks):
-        for kind in (TO_LOW, TO_HIGH, TO_UNDER, TO_OVER, OWN):
-            raw_copy(kind, r).start()
-
-    for copy in locals_:
-        copy.wait()
+    with scope("S_barrier"):
+        pl.semaphore_wait(barrier, count)
+
+    for kind in (TO_HIGH, OWN, TO_OVER):
+
+        @pl.when(exists[kind] & leads[kind])
+        def _(kind=kind):
+            pl.semaphore_signal(ready, inc=1, device_id=targets[kind], device_id_type=MESH)
+
+    locals_[0].wait()
+    for kind in (TO_LOW, TO_HIGH, TO_UNDER, TO_OVER, OWN):
+
+        @pl.when(exists[kind] & jnp.logical_not(late[kind]))
+        def _(kind=kind):
+            for r in range(chunks):
+                raw_copy(kind, r).start()
+
+    def clear(condition, refs):
+        @pl.when(jnp.logical_not(condition))
+        def _():
+            for ref in refs:
+                ref[...] = jnp.zeros(ref.shape, ref.dtype)
+
+    flat_z = [ref for a in range(2) for ref in summed_z[a]]
+    flat_y = [ref for a in range(2) for ref in summed_y[a]]
+    clear(has_low, [ref.at[0:2] for ref in raw_z + flat_z])
+    clear(has_high, [ref.at[6:8] for ref in raw_z + flat_z])
+    clear(has_under, [ref.at[0] for ref in raw_y + flat_y])
+    clear(has_over, [ref.at[1] for ref in raw_y + flat_y])
+
+    with scope("S_localwait"):
+        for copy in locals_[1:]:
+            copy.wait()
 
     clusters = 2 * atom_devices
     first_energy = 2 * d
@@ -178,8 +250,8 @@
     up_slot, down_slot, up_factor, down_factor = [], [], [], []
     for e in range(2):
         u, l = up[e], down[e]
-        up_slot.append(jnp.minimum(jnp.maximum(u - first_energy + 2, 4), 7))
-        down_slot.append(jnp.minimum(jnp.maximum(l - first_energy + 4, 0), 3))
+        up_slot.append(jnp.where(u >= 0, jnp.minimum(jnp.maximum(u - first_energy + 2, 4), 7), 7))
+        down_slot.append(jnp.where(l >= 0, jnp.minimum(jnp.maximum(l - first_energy + 4, 0), 3), 0))
         up_factor.append(jnp.where(u >= 0, up_weight[e], jnp.float32(0.0)))
         down_factor.append(jnp.where(l >= 0, down_weight[e], jnp.float32(0.0)))
 
@@ -235,47 +307,139 @@
             sent_y[0][r][1, e] = (reach[2, 0] * values[0] + reach[2, 1] * values[1]).astype(BF16)
             sent_y[1][r][1, e] = (reach[3, 1] * values[1]).astype(BF16)
 
-    def energy_sum_send(a, r):
-        for kind in (TO_UNDER, TO_OVER):
-            sum_copy(kind, a, r).start()
-
-    def cluster_sum_send(a, r):
-        for kind in (TO_LOW, TO_HIGH, OWN):
-            sum_copy(kind, a, r).start()
-
-    def raw_second(r):
-        raw_copy(OWN, r).wait_recv()
-        raw_copy(PASSED, r).wait_recv()
+    def start_sums(kinds, a, r, only=None):
+        for kind in kinds:
+            condition = exists[kind]
+            if only is not None:
+                condition = late[kind] if only else condition & jnp.logical_not(late[kind])
+
+            @pl.when(condition)
+            def _(kind=kind):
+                sum_copy(kind, a, r).start()
+
+    def pass_raw(r, whose=None):
+        @pl.when(pass_out if whose is None else pass_out & (core == whose))
+        def _():
+            with scope(f"W_zraw{r}"):
+                raw_arrival(r, passed_from, core).wait_recv()
+            raw_copy(PASSED, r).start()
+
+    def over_energies(r, only=None):
+        with scope(f"W_own{r}"):
+            raw_copy(OWN, r).wait_recv()
+
+        @pl.when(pass_in)
+        def _():
+            with scope(f"W_pass{r}"):
+                raw_arrival(r, kept_from, 1 - core).wait_recv()
+                raw_copy(PASSED, r).wait_recv()
+
         energy_sums(r)
-        energy_sum_send(0, r)
-
-    for r in range(chunks):
-        raw_copy(TO_LOW, r).wait_recv()
-        raw_copy(TO_HIGH, r).wait_recv()
-        raw_copy(PASSED, r).start()
-        if r:
-            raw_second(r - 1)
-        raw_copy(TO_UNDER, r).wait_recv()
-        raw_copy(TO_OVER, r).wait_recv()
+        start_sums(OVER_Y, 0, r, only)
+
+    def over_clusters(r, only=None):
+        with scope(f"W_yraw{r}"):
+
+            @pl.when(has_over)
+            def _():
+                raw_copy(TO_UNDER, r).wait_recv()
+
+            @pl.when(has_under)
+            def _():
+                raw_copy(TO_OVER, r).wait_recv()
+
         cluster_sums(r)
-        cluster_sum_send(0, r)
-    for r in range(chunks):
-        cluster_sum_send(1, r)
-    raw_second(chunks - 1)
-    for r in range(chunks):
-        energy_sum_send(1, r)
+        start_sums(OVER_Z, 0, r, only)
+
+    def meet(kinds):
+        pl.semaphore_wait(ready, 1)
+        for kind in kinds:
+
+            @pl.when(late[kind])
+            def _(kind=kind):
+                for r in range(chunks):
+                    raw_copy(kind, r).start()
+
+    @pl.when(jnp.logical_not(late_y | late_z))
+    def _():
+        for r in range(chunks):
+            pass_raw(r)
+            if r:
+                over_energies(r - 1)
+            over_clusters(r)
+        for r in range(chunks):
+            start_sums(OVER_Z, 1, r)
+        start_sums(OVER_Y, 1, 0)
+        over_energies(chunks - 1)
+        for r in range(1, chunks):
+            start_sums(OVER_Y, 1, r)
+
+    @pl.when(late_y)
+    def _():
+        for r in range(chunks):
+            pass_raw(r)
+            if r:
+                over_energies(r - 1, False)
+                if r == 1:
+                    meet(OVER_Y)
+                start_sums(OVER_Y, 0, r - 1, True)
+        start_sums(OVER_Y, 1, 0)
+        over_energies(chunks - 1)
+        for r in range(1, chunks):
+            start_sums(OVER_Y, 1, r)
+        for r in range(chunks):
+            over_clusters(r)
+        for r in range(chunks):
+            start_sums(OVER_Z, 1, r)
+
+    @pl.when(late_z)
+    def _():
+        for r in range(chunks):
+            pass_raw(r, early_core)
+            over_clusters(r, False)
+            if r == 0:
+
+                @pl.when(meets_z)
+                def _():
+                    meet(OVER_Z)
+
+            start_sums(OVER_Z, 0, r, True)
+        for r in range(chunks):
+            start_sums(OVER_Z, 1, r)
+        for r in range(chunks):
+            pass_raw(r, 1 - early_core)
+            if r:
+                over_energies(r - 1)
+        start_sums(OVER_Y, 1, 0)
+        over_energies(chunks - 1)
+        for r in range(1, chunks):
+            start_sums(OVER_Y, 1, r)
 
     def read(a, r):
         span = pl.ds(r * rows, rows)
-        for kind in (TO_UNDER, TO_OVER):
-            sum_copy(kind, a, r).wait_recv()
+        with scope(f"W_ysum{a}{r}"):
+
+            @pl.when(has_over)
+            def _():
+                sum_copy(TO_UNDER, a, r).wait_recv()
+
+            @pl.when(has_under)
+            def _():
+                sum_copy(TO_OVER, a, r).wait_recv()
+
         for e in range(2):
             total = wide(summed_y[a][r][0, e]) + wide(summed_y[a][r][1, e])
             for c in range(2):
                 total = total + reach[a, c] * wide(hidden[r][e, c])
             reader[a, e, :, 0:orbitals] = total.astype(BF16)
-        for kind in (OWN, PASSED):
-            sum_copy(kind, a, r).wait_recv()
+        with scope(f"W_zpass{a}{r}"):
+            sum_copy(OWN, a, r).wait_recv()
+
+            @pl.when(pass_in)
+            def _():
+                sum_arrival(a, r, kept_from, 1 - core).wait_recv()
+                sum_copy(PASSED, a, r).wait_recv()
+
         for e in range(2):
             total = up_factor[e] * wide(summed_z[a][r][up_slot[e]]) + down_factor[e] * wide(
                 summed_z[a][r][down_slot[e]]
@@ -304,35 +468,36 @@
             third = dot(second_cat[e].astype(BF16), f_big[e])
             for part in range(2):
                 side = slice(part * orbitals, (part + 1) * orbitals)
-                result[a, e, part] = (
+                out_ref[e, a, part] = (
                     wide(green[e, a, part]) + second_cat[e, :, side] + third[:, side]
                 ).astype(BF16)
-        for e in range(2):
-            out_copy(a, e).start()
-
-    def out_copy(a, e):
-        return pltpu.make_async_copy(result.at[a, e], out_hbm.at[e, a], out_sem.at[a, e])
 
     steps = [(a, r) for a in range(2) for r in range(chunks)]
     for at, (a, r) in enumerate(steps):
-        sum_copy(TO_LOW, a, r).wait_recv()
-        sum_copy(TO_HIGH, a, r).wait_recv()
-        sum_copy(PASSED, a, r).start()
+
+        @pl.when(pass_out)
+        def _(a=a, r=r):
+            with scope(f"W_zsum{a}{r}"):
+                sum_arrival(a, r, passed_from, core).wait_recv()
+            sum_copy(PASSED, a, r).start()
+
         if at:
             read(*steps[at - 1])
             if steps[at - 1][1] == chunks - 1:
                 finish(steps[at - 1][0])
     read(*steps[-1])
-    finish(1)
-
-    for r in range(chunks):
+    with scope("S_finish1"):
+        finish(1)
+
+    with scope("S_sends"):
         for kind in range(6):
-            raw_copy(kind, r).wait_send()
-            for a in range(2):
-                sum_copy(kind, a, r).wait_send()
-    for a in range(2):
-        for e in range(2):
-            out_copy(a, e).wait()
+
+            @pl.when(pass_out if kind == PASSED else exists[kind])
+            def _(kind=kind):
+                for r in range(chunks):
+                    raw_copy(kind, r).wait_send()
+                    for a in range(2):
+                        sum_copy(kind, a, r).wait_send()
 
 
 def solution(mesh):
@@ -373,34 +538,38 @@
                 vmem(2, 2, 2 * orbitals, 2 * orbitals),
                 vmem(2, 2 * orbitals, 2 * orbitals),
                 vmem(2, orbitals, 2 * orbitals, dtype=F32),
-                vmem(2, 2, 2, orbitals, orbitals),
                 pltpu.SemaphoreType.DMA((6, CHUNKS)),
                 pltpu.SemaphoreType.DMA((6, CHUNKS)),
                 pltpu.SemaphoreType.DMA((6, 2 * CHUNKS)),
                 pltpu.SemaphoreType.DMA((6, 2 * CHUNKS)),
                 pltpu.SemaphoreType.DMA((8,)),
-                pltpu.SemaphoreType.DMA((2, 2)),
+                pltpu.SemaphoreType.REGULAR,
             ]
         )
         return pl.pallas_call(
             functools.partial(kernel, energy_devices, atom_devices),
             out_shape=jax.ShapeDtypeStruct(green_blocks.shape, green_blocks.dtype),
             in_specs=[pl.BlockSpec(memory_space=pl.ANY)] * 8,
-            out_specs=pl.BlockSpec(memory_space=pl.ANY),
+            out_specs=pl.BlockSpec(memory_space=pltpu.VMEM),
             scratch_shapes=scratch,
             compiler_params=pltpu.CompilerParams(
-                collective_id=0, has_side_effects=True, vmem_limit_bytes=60 * 1024 * 1024
+                collective_id=0, has_side_effects=True, vmem_limit_bytes=24 * 1024 * 1024
             ),
             name="update",
         )(
-            green_blocks,
-            coupling,
-            up_partner,
-            down_partner,
-            up_weight,
-            down_weight,
-            neighbours.T,
-            strength.T,
+            *(
+                pltpu.with_memory_space_constraint(array, pltpu.HBM)
+                for array in (
+                    green_blocks,
+                    coupling,
+                    up_partner,
+                    down_partner,
+                    up_weight,
+                    down_weight,
+                    neighbours.T,
+                    strength.T,
+                )
+            )
         )
 
     in_specs = (

time: 50.1 us -> 43.1 us (0.86)
  the two profiles are of different devices: /device:TPU:1 before, /device:TPU:30 now
where the time goes in v2:
time: 43.1 us; the launch traced here: 42.9 us
  Pallas kernels  41.9 us (97%)
  local copies, waits for them, and re-layouts  0.97 us (2%)
    pallas_call x1, Pallas kernels, on_device(): pl.pallas_call(functools.partial(kernel, energy_devices, atom_devices), o...  41.9 us
    unnamed x1, local copies, waits for them, and re-layouts  0.97 us

profile of v2, /device:TPU:30, one launch (start us, length us, event | category | flops | bytes accessed | tf_op | source)
XLA Modules:
  0.0 42.9 jit_solution(391189216977318746)
XLA Ops:
  0.0 41.9 %update.1 = bf16[2,2,2,256,256]{4,3,2,1,0:T(8,128)(2,1)S(1)} custom-call(bf16[2,2,2,256,256]{4,3,2,1,0:T(8,128)(2,1)} %green_hbm.1, bf16[2,256,256]{2,1,0:T(8,128)(2,1)} %coupling_hbm.1, s32[2]{0:T(128)} %up_hbm.1, s32[2]{0:T(128)} %down_hbm.1, f32[2]{0:T(128)} %up_weight_hbm.1, f32[2]{0:T(128)} %down_weight_hbm.1, s32[5,16]{1,0:T(8,128)} %bitcast.2, ...), custom_call_target="tpu_custom_call" | custom-call | tf_op jit(solution)/shard_map/update/pallas_call | solution.py:549
  41.9 1.0 %copy.10 = bf16[2,2,2,256,256]{4,3,2,1,0:T(8,128)(2,1)} copy(bf16[2,2,2,256,256]{4,3,2,1,0:T(8,128)(2,1)S(1)} %update.1) | data formatting | bytes 2097152

commit v3 on v2

--- a/solution.py
+++ b/solution.py
@@ -47,6 +47,8 @@
     summed_y = [take(chunks) for _ in range(2)]
     own_sum = [take(chunks) for _ in range(2)]
     hidden = take(chunks)
+    relay_raw = dict(zip((chunks - 2, chunks - 1), take(2)))
+    relay_sum = [take(2) for _ in range(2)]
     sent_y = [take(chunks) for _ in range(2)]
     (
         green,
@@ -63,10 +65,11 @@
         y_big,
         f_big,
         second_cat,
-        raw_send,
+        sent,
         raw_recv,
-        sum_send,
         sum_recv,
+        relay_send,
+        relay_recv,
         local_sem,
         ready,
     ) = names
@@ -113,6 +116,24 @@
     slow_high = (place >= ROW - 2) & has_high
     late_z = meets_z | slow_high
     early_core = jnp.where(slow_high, 1, 0)
+    row = lax.div(d, ROW)
+    relays = (place >= ROW - 2) & (d >= ROW)
+    greets = (place < 2) & (d >= ROW)
+    detours_raw = {chunks - 1: 0, chunks - 2: 1}
+    detours_sum = {0: 0, 1: 2}
+
+    def detour(r):
+        return slow_high & (row >= detours_raw[r]) if r in detours_raw else never
+
+    def relayed(r):
+        return relays & (row >= detours_raw[r] + 1)
+
+    def detour_sum(r):
+        return slow_high & (row >= detours_sum[r]) if r in detours_sum else never
+
+    def relayed_sum(r):
+        return relays & (row >= detours_sum[r] + 1)
+
     late_y = late[TO_UNDER]
     pass_out = jnp.where(core == 0, d < energy_devices - 2, d >= 2)
     pass_in = jnp.where(core == 0, d >= 2, d < energy_devices - 2)
@@ -135,12 +156,12 @@
             dst_ref=target,
             send_sem=send,
             recv_sem=recv,
-            device_id=targets[kind],
+            device_id=targets[kind] if isinstance(kind, int) else kind,
             device_id_type=MESH,
         )
 
     def raw_copy(kind, r):
-        send, recv = raw_send.at[kind, r], raw_recv.at[kind, r]
+        send, recv = sent.at[kind], raw_recv.at[kind, r]
         if kind in (TO_UNDER, TO_OVER):
             source = green.at[:, :, 1, pl.ds(r * rows, rows), :]
             side = 1 if kind == TO_UNDER else 0
@@ -154,7 +175,7 @@
 
     def sum_copy(kind, a, r):
         index = a * chunks + r
-        send, recv = sum_send.at[kind, index], sum_recv.at[kind, index]
+        send, recv = sent.at[kind], sum_recv.at[kind, index]
         if kind in (TO_UNDER, TO_OVER):
             side = 1 if kind == TO_UNDER else 0
             return remote(
@@ -167,13 +188,53 @@
             source = own_sum[a][r]
         return remote(source, target, send, recv, kind)
 
+    def raw_detour(r):
+        source = green.at[:, :, 0, pl.ds(r * rows, rows), :]
+        send = sent.at[TO_HIGH]
+        return remote(source, relay_raw[r], send, relay_recv.at[chunks - 1 - r], (d + ROW, y))
+
+    def sum_detour(a, r):
+        index = a * chunks + r
+        send, recv = sent.at[TO_HIGH], relay_recv.at[2 + 2 * a + r]
+        return remote(own_sum[a][r], relay_sum[a][r], send, recv, (d + ROW, y))
+
+    def raw_relay(r):
+        target, recv = raw_z[r].at[0:2], raw_recv.at[TO_HIGH, r]
+        return remote(relay_raw[r], target, relay_send.at[chunks - 1 - r], recv, (d - ROW + 2, y))
+
+    def sum_relay(a, r):
+        index = a * chunks + r
+        send, recv = relay_send.at[2 + 2 * a + r], sum_recv.at[TO_HIGH, index]
+        return remote(relay_sum[a][r], summed_z[a][r].at[0:2], send, recv, (d - ROW + 2, y))
+
+    def relay_raw_step(r, condition):
+        @pl.when(condition)
+        def _():
+            raw_detour(r).wait_recv()
+            raw_relay(r).start()
+
+    def relay_step(at):
+        if at == 0:
+            relay_raw_step(chunks - 2, relays & (row >= 2))
+            relay_raw_step(chunks - 1, relays & (row == 1))
+        if at == 1:
+            relay_raw_step(chunks - 1, relays & (row >= 2))
+        if at - 2 in detours_sum:
+            r = at - 2
+
+            @pl.when(relayed_sum(r))
+            def _():
+                for a in range(2):
+                    sum_detour(a, r).wait_recv()
+                    sum_relay(a, r).start()
+
     def raw_arrival(r, start, which):
         place = raw_z[r].at[pl.ds(start, 2)]
-        return remote(place, place, raw_send.at[which, r], raw_recv.at[which, r], OWN)
+        return remote(place, place, sent.at[which], raw_recv.at[which, r], OWN)
 
     def sum_arrival(a, r, start, which):
         place, index = summed_z[a][r].at[pl.ds(start, 2)], a * chunks + r
-        return remote(place, place, sum_send.at[which, index], sum_recv.at[which, index], OWN)
+        return remote(place, place, sent.at[which], sum_recv.at[which, index], OWN)
 
     locals_ = [
         pltpu.make_async_copy(source, target, local_sem.at[i])
@@ -193,6 +254,15 @@
     for copy in locals_:
         copy.start()
 
+    @pl.when(greets)
+    def _():
+        pl.semaphore_signal(barrier, inc=1, device_id=(d + ROW - 2, y), device_id_type=MESH)
+
+    @pl.when(relays)
+    def _():
+        pl.semaphore_signal(barrier, inc=1, device_id=(d - ROW, y), device_id_type=MESH)
+
+    count = count + jnp.where(relays, 1, 0) + jnp.where(slow_high, 1, 0)
     with scope("S_barrier"):
         pl.semaphore_wait(barrier, count)
 
@@ -208,7 +278,17 @@
         @pl.when(exists[kind] & jnp.logical_not(late[kind]))
         def _(kind=kind):
             for r in range(chunks):
-                raw_copy(kind, r).start()
+                if kind != TO_HIGH or r not in detours_raw:
+                    raw_copy(kind, r).start()
+                    continue
+
+                @pl.when(detour(r))
+                def _(r=r):
+                    raw_detour(r).start()
+
+                @pl.when(jnp.logical_not(detour(r)))
+                def _(r=r):
+                    raw_copy(TO_HIGH, r).start()
 
     def clear(condition, refs):
         @pl.when(jnp.logical_not(condition))
@@ -312,6 +392,8 @@
             condition = exists[kind]
             if only is not None:
                 condition = late[kind] if only else condition & jnp.logical_not(late[kind])
+            if kind == TO_HIGH and r in detours_sum and only is not True:
+                condition = condition & jnp.logical_not(detour_sum(r))
 
             @pl.when(condition)
             def _(kind=kind):
@@ -367,6 +449,7 @@
             if r:
                 over_energies(r - 1)
             over_clusters(r)
+            relay_step(r)
         for r in range(chunks):
             start_sums(OVER_Z, 1, r)
         start_sums(OVER_Y, 1, 0)
@@ -403,9 +486,16 @@
                 def _():
                     meet(OVER_Z)
 
+            if r in detours_sum:
+
+                @pl.when(detour_sum(r))
+                def _(r=r):
+                    for a in range(2):
+                        sum_detour(a, r).start()
+
             start_sums(OVER_Z, 0, r, True)
-        for r in range(chunks):
             start_sums(OVER_Z, 1, r)
+            relay_step(r)
         for r in range(chunks):
             pass_raw(r, 1 - early_core)
             if r:
@@ -472,15 +562,21 @@
                     wide(green[e, a, part]) + second_cat[e, :, side] + third[:, side]
                 ).astype(BF16)
 
-    steps = [(a, r) for a in range(2) for r in range(chunks)]
-    for at, (a, r) in enumerate(steps):
-
-        @pl.when(pass_out)
-        def _(a=a, r=r):
+    def pass_sum(a, r, condition):
+        @pl.when(condition)
+        def _():
             with scope(f"W_zsum{a}{r}"):
                 sum_arrival(a, r, passed_from, core).wait_recv()
             sum_copy(PASSED, a, r).start()
 
+    steps = [(a, r) for a in range(2) for r in range(chunks)]
+    for at, (a, r) in enumerate(steps):
+        pass_sum(a, r, pass_out if at <= chunks else pass_out & jnp.logical_not(greets))
+        if at == chunks:
+            for ahead in range(1, chunks - 1):
+                pass_sum(1, ahead, pass_out & greets)
+        if at == chunks + 1:
+            pass_sum(1, chunks - 1, pass_out & greets)
         if at:
             read(*steps[at - 1])
             if steps[at - 1][1] == chunks - 1:
@@ -494,10 +590,20 @@
 
             @pl.when(pass_out if kind == PASSED else exists[kind])
             def _(kind=kind):
-                for r in range(chunks):
-                    raw_copy(kind, r).wait_send()
-                    for a in range(2):
-                        sum_copy(kind, a, r).wait_send()
+                remote(green, green, sent.at[kind], raw_recv.at[kind, 0], OWN).wait_send()
+
+        for r in detours_raw:
+
+            @pl.when(relayed(r))
+            def _(r=r):
+                raw_relay(r).wait_send()
+
+        for r in detours_sum:
+
+            @pl.when(relayed_sum(r))
+            def _(r=r):
+                for a in range(2):
+                    sum_relay(a, r).wait_send()
 
 
 def solution(mesh):
@@ -522,6 +628,8 @@
             + [vmem(2, 2, rows, orbitals) for _ in range(2 * CHUNKS)]
             + [vmem(2, rows, orbitals) for _ in range(2 * CHUNKS)]
             + [vmem(2, 2, rows, orbitals) for _ in many]
+            + [vmem(2, 2, rows, orbitals) for _ in range(2)]
+            + [vmem(2, rows, orbitals) for _ in range(4)]
             + [vmem(2, 2, rows, orbitals) for _ in range(2 * CHUNKS)]
             + [
                 vmem(2, 2, 2, orbitals, orbitals),
@@ -538,10 +646,11 @@
                 vmem(2, 2, 2 * orbitals, 2 * orbitals),
                 vmem(2, 2 * orbitals, 2 * orbitals),
                 vmem(2, orbitals, 2 * orbitals, dtype=F32),
-                pltpu.SemaphoreType.DMA((6, CHUNKS)),
+                pltpu.SemaphoreType.DMA((6,)),
                 pltpu.SemaphoreType.DMA((6, CHUNKS)),
                 pltpu.SemaphoreType.DMA((6, 2 * CHUNKS)),
-                pltpu.SemaphoreType.DMA((6, 2 * CHUNKS)),
+                pltpu.SemaphoreType.DMA((6,)),
+                pltpu.SemaphoreType.DMA((6,)),
                 pltpu.SemaphoreType.DMA((8,)),
                 pltpu.SemaphoreType.REGULAR,
             ]

time: 43.1 us -> 41.6 us (0.965)
  the two profiles are of different devices: /device:TPU:30 before, /device:TPU:23 now
where the time goes in v3:
time: 41.6 us; the launch traced here: 41.5 us
  Pallas kernels  40.5 us (97%)
  local copies, waits for them, and re-layouts  0.97 us (2%)
    pallas_call x1, Pallas kernels, on_device(): pl.pallas_call(functools.partial(kernel, energy_devices, atom_devices), o...  40.5 us
    unnamed x1, local copies, waits for them, and re-layouts  0.97 us

profile of v3, /device:TPU:23, one launch (start us, length us, event | category | flops | bytes accessed | tf_op | source)
XLA Modules:
  0.0 41.5 jit_solution(18211849334074042508)
XLA Ops:
  0.0 40.5 %update.1 = bf16[2,2,2,256,256]{4,3,2,1,0:T(8,128)(2,1)S(1)} custom-call(bf16[2,2,2,256,256]{4,3,2,1,0:T(8,128)(2,1)} %green_hbm.1, bf16[2,256,256]{2,1,0:T(8,128)(2,1)} %coupling_hbm.1, s32[2]{0:T(128)} %up_hbm.1, s32[2]{0:T(128)} %down_hbm.1, f32[2]{0:T(128)} %up_weight_hbm.1, f32[2]{0:T(128)} %down_weight_hbm.1, s32[5,16]{1,0:T(8,128)} %bitcast.2, ...), custom_call_target="tpu_custom_call" | custom-call | tf_op jit(solution)/shard_map/update/pallas_call | solution.py:658
  40.5 1.0 %copy.10 = bf16[2,2,2,256,256]{4,3,2,1,0:T(8,128)(2,1)} copy(bf16[2,2,2,256,256]{4,3,2,1,0:T(8,128)(2,1)S(1)} %update.1) | data formatting | bytes 2097152

commit v4 on v3

--- a/solution.py
+++ b/solution.py
@@ -387,9 +387,9 @@
             sent_y[0][r][1, e] = (reach[2, 0] * values[0] + reach[2, 1] * values[1]).astype(BF16)
             sent_y[1][r][1, e] = (reach[3, 1] * values[1]).astype(BF16)
 
-    def start_sums(kinds, a, r, only=None):
+    def start_sums(kinds, a, r, only=None, extra=None):
         for kind in kinds:
-            condition = exists[kind]
+            condition = exists[kind] if extra is None else exists[kind] & extra
             if only is not None:
                 condition = late[kind] if only else condition & jnp.logical_not(late[kind])
             if kind == TO_HIGH and r in detours_sum and only is not True:
@@ -500,10 +500,13 @@
             pass_raw(r, 1 - early_core)
             if r:
                 over_energies(r - 1)
-        start_sums(OVER_Y, 1, 0)
+                start_sums(OVER_Y, 1, r - 1, extra=greets)
+        others = jnp.logical_not(greets)
+        start_sums(OVER_Y, 1, 0, extra=others)
         over_energies(chunks - 1)
-        for r in range(1, chunks):
-            start_sums(OVER_Y, 1, r)
+        for r in range(1, chunks - 1):
+            start_sums(OVER_Y, 1, r, extra=others)
+        start_sums(OVER_Y, 1, chunks - 1)
 
     def read(a, r):
         span = pl.ds(r * rows, rows)
@@ -569,20 +572,44 @@
                 sum_arrival(a, r, passed_from, core).wait_recv()
             sum_copy(PASSED, a, r).start()
 
-    steps = [(a, r) for a in range(2) for r in range(chunks)]
-    for at, (a, r) in enumerate(steps):
-        pass_sum(a, r, pass_out if at <= chunks else pass_out & jnp.logical_not(greets))
-        if at == chunks:
-            for ahead in range(1, chunks - 1):
-                pass_sum(1, ahead, pass_out & greets)
-        if at == chunks + 1:
-            pass_sum(1, chunks - 1, pass_out & greets)
-        if at:
-            read(*steps[at - 1])
-            if steps[at - 1][1] == chunks - 1:
-                finish(steps[at - 1][0])
-    read(*steps[-1])
-    with scope("S_finish1"):
+    @pl.when(jnp.logical_not(greets))
+    def _():
+        steps = [(a, r) for a in range(2) for r in range(chunks)]
+        for at, (a, r) in enumerate(steps):
+            pass_sum(a, r, pass_out)
+            if at:
+                read(*steps[at - 1])
+                if steps[at - 1][1] == chunks - 1:
+                    finish(steps[at - 1][0])
+        read(*steps[-1])
+        finish(1)
+
+    @pl.when(greets)
+    def _():
+        last = chunks - 1
+        lower, upper = pass_out & (core == 0), pass_out & (core == 1)
+
+        @pl.when(lower)
+        def _():
+            for a in range(2):
+                for r in range(chunks):
+                    sum_arrival(a, r, passed_from, core).wait_recv()
+                    sum_copy(PASSED, a, r).start()
+
+        for r in range(1, last):
+            for a in range(2):
+                pass_sum(a, r, upper)
+            for a in range(2):
+                read(a, r)
+        for a in range(2):
+            pass_sum(a, 0, upper)
+        read(0, 0)
+        pass_sum(0, last, upper)
+        read(1, 0)
+        pass_sum(1, last, upper)
+        read(0, last)
+        finish(0)
+        read(1, last)
         finish(1)
 
     with scope("S_sends"):

time: 41.6 us -> 40.7 us (0.978)
  the two profiles are of different devices: /device:TPU:23 before, /device:TPU:30 now
where the time goes in v4:
time: 40.7 us; the launch traced here: 40.5 us
  Pallas kernels  39.5 us (97%)
  local copies, waits for them, and re-layouts  0.97 us (2%)
    pallas_call x1, Pallas kernels, on_device(): pl.pallas_call(functools.partial(kernel, energy_devices, atom_devices), o...  39.5 us
    unnamed x1, local copies, waits for them, and re-layouts  0.97 us

profile of v4, /device:TPU:30, one launch (start us, length us, event | category | flops | bytes accessed | tf_op | source)
XLA Modules:
  0.0 40.5 jit_solution(2307982030324180839)
XLA Ops:
  0.0 39.5 %update.1 = bf16[2,2,2,256,256]{4,3,2,1,0:T(8,128)(2,1)S(1)} custom-call(bf16[2,2,2,256,256]{4,3,2,1,0:T(8,128)(2,1)} %green_hbm.1, bf16[2,256,256]{2,1,0:T(8,128)(2,1)} %coupling_hbm.1, s32[2]{0:T(128)} %up_hbm.1, s32[2]{0:T(128)} %down_hbm.1, f32[2]{0:T(128)} %up_weight_hbm.1, f32[2]{0:T(128)} %down_weight_hbm.1, s32[5,16]{1,0:T(8,128)} %bitcast.2, ...), custom_call_target="tpu_custom_call" | custom-call | tf_op jit(solution)/shard_map/update/pallas_call | solution.py:685
  39.5 1.0 %copy.10 = bf16[2,2,2,256,256]{4,3,2,1,0:T(8,128)(2,1)} copy(bf16[2,2,2,256,256]{4,3,2,1,0:T(8,128)(2,1)S(1)} %update.1) | data formatting | bytes 2097152

commit v5 on v4

--- a/solution.py
+++ b/solution.py
@@ -14,6 +14,7 @@
 BF16 = jnp.bfloat16
 
 TO_LOW, TO_HIGH, OWN, PASSED, TO_UNDER, TO_OVER = range(6)
+ARRIVAL = (0, 1, 2, 2, 3, 3)
 OVER_Z = (TO_LOW, TO_HIGH, OWN)
 OVER_Y = (TO_UNDER, TO_OVER)
 scope = jax.named_scope
@@ -161,7 +162,7 @@
         )
 
     def raw_copy(kind, r):
-        send, recv = sent.at[kind], raw_recv.at[kind, r]
+        send, recv = sent.at[kind], raw_recv.at[ARRIVAL[kind], r]
         if kind in (TO_UNDER, TO_OVER):
             source = green.at[:, :, 1, pl.ds(r * rows, rows), :]
             side = 1 if kind == TO_UNDER else 0
@@ -175,7 +176,7 @@
 
     def sum_copy(kind, a, r):
         index = a * chunks + r
-        send, recv = sent.at[kind], sum_recv.at[kind, index]
+        send, recv = sent.at[kind], sum_recv.at[ARRIVAL[kind], index]
         if kind in (TO_UNDER, TO_OVER):
             side = 1 if kind == TO_UNDER else 0
             return remote(
@@ -227,6 +228,12 @@
                 for a in range(2):
                     sum_detour(a, r).wait_recv()
                     sum_relay(a, r).start()
+
+    def together(place, recv):
+        remote(place, place, sent.at[OWN], recv, OWN).wait_recv()
+
+    both_y = has_under & has_over
+    single_y = (has_under | has_over) & jnp.logical_not(both_y)
 
     def raw_arrival(r, start, which):
         place = raw_z[r].at[pl.ds(start, 2)]
@@ -407,14 +414,15 @@
             raw_copy(PASSED, r).start()
 
     def over_energies(r, only=None):
-        with scope(f"W_own{r}"):
+        @pl.when(jnp.logical_not(pass_in))
+        def _():
             raw_copy(OWN, r).wait_recv()
 
         @pl.when(pass_in)
         def _():
             with scope(f"W_pass{r}"):
                 raw_arrival(r, kept_from, 1 - core).wait_recv()
-                raw_copy(PASSED, r).wait_recv()
+                together(raw_z[r].at[2:6], raw_recv.at[2, r])
 
         energy_sums(r)
         start_sums(OVER_Y, 0, r, only)
@@ -422,11 +430,11 @@
     def over_clusters(r, only=None):
         with scope(f"W_yraw{r}"):
 
-            @pl.when(has_over)
+            @pl.when(both_y)
             def _():
-                raw_copy(TO_UNDER, r).wait_recv()
-
-            @pl.when(has_under)
+                together(raw_y[r], raw_recv.at[3, r])
+
+            @pl.when(single_y)
             def _():
                 raw_copy(TO_OVER, r).wait_recv()
 
@@ -512,11 +520,11 @@
         span = pl.ds(r * rows, rows)
         with scope(f"W_ysum{a}{r}"):
 
-            @pl.when(has_over)
+            @pl.when(both_y)
             def _():
-                sum_copy(TO_UNDER, a, r).wait_recv()
-
-            @pl.when(has_under)
+                together(summed_y[a][r], sum_recv.at[3, a * chunks + r])
+
+            @pl.when(single_y)
             def _():
                 sum_copy(TO_OVER, a, r).wait_recv()
 
@@ -526,12 +534,15 @@
                 total = total + reach[a, c] * wide(hidden[r][e, c])
             reader[a, e, :, 0:orbitals] = total.astype(BF16)
         with scope(f"W_zpass{a}{r}"):
-            sum_copy(OWN, a, r).wait_recv()
+
+            @pl.when(jnp.logical_not(pass_in))
+            def _():
+                sum_copy(OWN, a, r).wait_recv()
 
             @pl.when(pass_in)
             def _():
                 sum_arrival(a, r, kept_from, 1 - core).wait_recv()
-                sum_copy(PASSED, a, r).wait_recv()
+                together(summed_z[a][r].at[2:6], sum_recv.at[2, a * chunks + r])
 
         for e in range(2):
             total = up_factor[e] * wide(summed_z[a][r][up_slot[e]]) + down_factor[e] * wide(
@@ -617,7 +628,7 @@
 
             @pl.when(pass_out if kind == PASSED else exists[kind])
             def _(kind=kind):
-                remote(green, green, sent.at[kind], raw_recv.at[kind, 0], OWN).wait_send()
+                remote(green, green, sent.at[kind], raw_recv.at[0, 0], OWN).wait_send()
 
         for r in detours_raw:
 
@@ -674,8 +685,8 @@
                 vmem(2, 2 * orbitals, 2 * orbitals),
                 vmem(2, orbitals, 2 * orbitals, dtype=F32),
                 pltpu.SemaphoreType.DMA((6,)),
-                pltpu.SemaphoreType.DMA((6, CHUNKS)),
-                pltpu.SemaphoreType.DMA((6, 2 * CHUNKS)),
+                pltpu.SemaphoreType.DMA((4, CHUNKS)),
+                pltpu.SemaphoreType.DMA((4, 2 * CHUNKS)),
                 pltpu.SemaphoreType.DMA((6,)),
                 pltpu.SemaphoreType.DMA((6,)),
                 pltpu.SemaphoreType.DMA((8,)),

time: 40.7 us -> 40.5 us (level)
  no operation moved by 1% of the time
where the time goes in v5:
time: 40.5 us; the launch traced here: 40.3 us
  Pallas kernels  39.3 us (97%)
  local copies, waits for them, and re-layouts  0.97 us (2%)
    pallas_call x1, Pallas kernels, on_device(): pl.pallas_call(functools.partial(kernel, energy_devices, atom_devices), o...  39.3 us
    unnamed x1, local copies, waits for them, and re-layouts  0.97 us

profile of v5, /device:TPU:30, one launch (start us, length us, event | category | flops | bytes accessed | tf_op | source)
XLA Modules:
  0.0 40.3 jit_solution(14184025245475579046)
XLA Ops:
  0.0 39.3 %update.1 = bf16[2,2,2,256,256]{4,3,2,1,0:T(8,128)(2,1)S(1)} custom-call(bf16[2,2,2,256,256]{4,3,2,1,0:T(8,128)(2,1)} %green_hbm.1, bf16[2,256,256]{2,1,0:T(8,128)(2,1)} %coupling_hbm.1, s32[2]{0:T(128)} %up_hbm.1, s32[2]{0:T(128)} %down_hbm.1, f32[2]{0:T(128)} %up_weight_hbm.1, f32[2]{0:T(128)} %down_weight_hbm.1, s32[5,16]{1,0:T(8,128)} %bitcast.2, ...), custom_call_target="tpu_custom_call" | custom-call | tf_op jit(solution)/shard_map/update/pallas_call | solution.py:696
  39.3 1.0 %copy.10 = bf16[2,2,2,256,256]{4,3,2,1,0:T(8,128)(2,1)} copy(bf16[2,2,2,256,256]{4,3,2,1,0:T(8,128)(2,1)S(1)} %update.1) | data formatting | bytes 2097152

commit v6 on v5

--- a/solution.py
+++ b/solution.py
@@ -280,7 +280,7 @@
             pl.semaphore_signal(ready, inc=1, device_id=targets[kind], device_id_type=MESH)
 
     locals_[0].wait()
-    for kind in (TO_LOW, TO_HIGH, TO_UNDER, TO_OVER, OWN):
+    for kind in (TO_UNDER, TO_OVER, TO_HIGH, TO_LOW, OWN):
 
         @pl.when(exists[kind] & jnp.logical_not(late[kind]))
         def _(kind=kind):

time: 40.5 us -> 40.5 us (level)
  no operation moved by 1% of the time
where the time goes in v6:
time: 40.5 us; the launch traced here: 40.3 us
  Pallas kernels  39.3 us (97%)
  local copies, waits for them, and re-layouts  0.97 us (2%)
    pallas_call x1, Pallas kernels, on_device(): pl.pallas_call(functools.partial(kernel, energy_devices, atom_devices), o...  39.3 us
    unnamed x1, local copies, waits for them, and re-layouts  0.97 us

profile of v6, /device:TPU:30, one launch (start us, length us, event | category | flops | bytes accessed | tf_op | source)
XLA Modules:
  0.0 40.3 jit_solution(14895709474526398702)
XLA Ops:
  0.0 39.3 %update.1 = bf16[2,2,2,256,256]{4,3,2,1,0:T(8,128)(2,1)S(1)} custom-call(bf16[2,2,2,256,256]{4,3,2,1,0:T(8,128)(2,1)} %green_hbm.1, bf16[2,256,256]{2,1,0:T(8,128)(2,1)} %coupling_hbm.1, s32[2]{0:T(128)} %up_hbm.1, s32[2]{0:T(128)} %down_hbm.1, f32[2]{0:T(128)} %up_weight_hbm.1, f32[2]{0:T(128)} %down_weight_hbm.1, s32[5,16]{1,0:T(8,128)} %bitcast.2, ...), custom_call_target="tpu_custom_call" | custom-call | tf_op jit(solution)/shard_map/update/pallas_call | solution.py:696
  39.3 1.0 %copy.10 = bf16[2,2,2,256,256]{4,3,2,1,0:T(8,128)(2,1)} copy(bf16[2,2,2,256,256]{4,3,2,1,0:T(8,128)(2,1)S(1)} %update.1) | data formatting | bytes 2097152
